TPU v7x, 256 devices: a whole 4x4x8 slice. The times are simulated.
256 devices in a mesh: dp: 8 (over x, core), ctx: 32 (over y, z).
Axes of the slice: x: 4, y: 4, z: 8, core: 2. Of those that a mesh axis runs over, the one named last changes fastest.
Arguments:
- tokens: bfloat16 [32768, 4096], P(('dp', 'ctx')), parts along dimension 0, may hold values from -6 to 6
- pick_flags: int32 [32768], P(('dp', 'ctx')), parts along dimension 0, may hold values from 0 to 1, as said below
- gate_scales: bfloat16 [32768], P(('dp', 'ctx')), parts along dimension 0, may hold values from 0.099609375 to 1
- attn_gain: float32 [4096], replicated, may hold values from 0.4 to 1.6
- query_weight: bfloat16 [4096, 4096], P(None, 'ctx')
- key_weight: bfloat16 [4096, 1024], P(None, 'ctx')
- value_matrix: bfloat16 [4096, 1024], P(None, 'ctx'), may hold values from -0.09375 to 0.09375
- output_weight: bfloat16 [4096, 4096], P('ctx'), may hold values from -0.09375 to 0.09375
- ffn_gain: float32 [4096], replicated, may hold values from 0.25 to 1.75
- gate_weight: bfloat16 [4096, 11264], P(None, 'ctx'), may hold values from -0.09375 to 0.09375
- up_weight: bfloat16 [4096, 11264], P(None, 'ctx'), may hold values from -0.09375 to 0.09375
- down_weight: bfloat16 [11264, 4096], P('ctx'), may hold values from -0.0546875 to 0.0546875
Outputs:
- block_out: bfloat16 [32768, 4096], P(('dp', 'ctx')), parts along dimension 0
There are 8 independent parts, one for each index of `dp`. A program takes and returns all parts, laid end to end along the dimension named above; an argument that names none is the same for every part. Nothing has to cross between parts.
Inputs may be any that keep to these rules, and one draw needn't show every extreme that they name: `pick_flags`: each device's 128 tokens hold at most 32 picks, the first device exactly 32; each document holds exactly 512 picks; a device may hold none.
All inputs are finite; a program needn't handle non-finite values.
Results may differ from a plain program's by a relative error of at most 0.01.
Values may be sent and summed in bfloat16 or wider, within the bound.
A program may use at most 128 MiB of HBM per device.

v0:
```python
import jax
import jax.numpy as jnp
from jax import lax
from jax.sharding import PartitionSpec as P

QUERY_HEADS = 32
KEY_VALUE_HEADS = 8
HEAD_SIZE = 128
PICK_DEV = 16
MOST = 32
norm_eps = 1e-05
rope_base = 500000.0


def rms_scale(matrix, gain_vec):
    mean_square = jnp.mean(matrix * matrix, axis=-1, keepdims=True)
    return matrix * lax.rsqrt(mean_square + norm_eps) * gain_vec


def apply_rotary(values, token_positions):
    half_dim = values.shape[-1] // 2
    frequency = rope_base ** (-(jnp.arange(half_dim, dtype=jnp.float32) * 2.0) / values.shape[-1])
    angles = token_positions.astype(jnp.float32)[:, None] * frequency[None, :]
    cosine = jnp.cos(angles)
    sine_part = jnp.sin(angles)
    lower_half = values[..., :half_dim]
    upper_half = values[..., half_dim:]
    return jnp.concatenate(
        (
            lower_half * cosine - upper_half * sine_part,
            upper_half * cosine + lower_half * sine_part,
        ),
        axis=-1,
    )


def reduce_scatter_rows(partial, ctx_size):
    rows, width = partial.shape
    pieces = lax.all_to_all(
        partial.reshape(ctx_size, rows // ctx_size, width), "ctx", 0, 0, tiled=True
    )
    return jnp.sum(pieces.astype(jnp.float32), axis=0)


def body(
    tokens,
    pick_flags,
    gate_scales,
    attn_gain,
    query_weight,
    key_weight,
    value_matrix,
    output_weight,
    ffn_gain,
    gate_weight,
    up_weight,
    down_weight,
):
    tok_local, width = tokens.shape
    ctx_size = lax.axis_size("ctx")
    my_index = lax.axis_index("ctx")
    picked_count = PICK_DEV * ctx_size
    half_pick = PICK_DEV // 2
    half_cycle = ctx_size // 2
    slot_of = jnp.cumsum(pick_flags) - 1
    token_ids = jnp.arange(tok_local, dtype=jnp.int32)
    slot_match = (jnp.arange(MOST, dtype=jnp.int32)[:, None] == slot_of[None, :]) & (
        pick_flags[None, :] == 1
    )
    chosen = jnp.sum(jnp.where(slot_match, token_ids[None, :], 0), axis=1)
    filled = jnp.any(slot_match, axis=1)
    local_index = jnp.where(filled, chosen, -1)
    padded_rows = jnp.where(filled[:, None], tokens[chosen], jnp.zeros((), jnp.bfloat16))
    padded_gate = jnp.where(filled, gate_scales[chosen], jnp.zeros((), jnp.bfloat16))
    lane = jnp.arange(128, dtype=jnp.int32)[None, :]
    extra = jnp.where(
        lane == 0,
        local_index.astype(jnp.bfloat16)[:, None],
        jnp.where(lane == 1, padded_gate[:, None], jnp.zeros((), jnp.bfloat16)),
    )
    packed = jnp.concatenate((padded_rows, extra), axis=1)
    all_packed = lax.all_gather(packed, "ctx", axis=0, tiled=True)
    all_rows = all_packed[:, :width]
    all_index = all_packed[:, width].astype(jnp.int32)
    all_gate = all_packed[:, width + 1]
    counts = jnp.sum((all_index >= 0).reshape(ctx_size, MOST).astype(jnp.int32), axis=1)
    run_ends = jnp.cumsum(counts)
    run_starts = run_ends - counts
    order_ids = jnp.arange(picked_count, dtype=jnp.int32)
    owner_of = order_ids // PICK_DEV
    within = order_ids % PICK_DEV
    low_part = within < half_pick
    rank_block = jnp.where(low_part, owner_of, (owner_of + half_cycle) % ctx_size)
    rank_inner = jnp.where(low_part, 2 * within, 2 * (within - half_pick) + 1)
    rank_ids = rank_block * PICK_DEV + rank_inner
    source = jnp.sum((run_ends[None, :] <= rank_ids[:, None]).astype(jnp.int32), axis=1)
    flat_row = source * MOST + rank_ids - run_starts[source]
    picked_rows = all_rows[flat_row]
    scales = all_gate[flat_row].astype(jnp.float32)
    token_positions = source * tok_local + all_index[flat_row]
    normalized_rows = rms_scale(picked_rows.astype(jnp.float32), attn_gain).astype(jnp.bfloat16)
    queries = jnp.dot(normalized_rows, query_weight, preferred_element_type=jnp.float32)
    queries = apply_rotary(queries, token_positions).astype(jnp.bfloat16)
    kv_weight = jnp.concatenate((key_weight, value_matrix), axis=1)
    kv_local = jnp.einsum(
        "pd,dc->cp", normalized_rows, kv_weight, preferred_element_type=jnp.float32
    ).astype(jnp.bfloat16)
    comps = key_weight.shape[1] // KEY_VALUE_HEADS
    query_group_width = QUERY_HEADS // KEY_VALUE_HEADS
    by_head = jnp.transpose(kv_local.reshape(2, comps, KEY_VALUE_HEADS, picked_count), (2, 0, 1, 3))
    send = jnp.repeat(by_head, query_group_width, axis=0)
    got = lax.all_to_all(send, "ctx", 0, 0, tiled=True)
    key_cols = got[:, 0].reshape(ctx_size * comps, picked_count)
    value_cols = got[:, 1].reshape(ctx_size * comps, picked_count)
    keys_here = apply_rotary(key_cols.T.astype(jnp.float32), token_positions).astype(jnp.bfloat16)
    values_here = value_cols.T
    scores = jnp.dot(queries, keys_here.T, preferred_element_type=jnp.float32) / jnp.sqrt(
        jnp.float32(HEAD_SIZE)
    )
    allowed = token_positions[None, :] <= token_positions[:, None]
    scores = jnp.where(allowed, scores, -jnp.inf)
    row_max = jnp.max(scores, axis=1, keepdims=True)
    exp_terms = jnp.exp(scores - row_max)
    prob_bf = (exp_terms / jnp.sum(exp_terms, axis=1, keepdims=True)).astype(jnp.bfloat16)
    head_out = jnp.dot(prob_bf, values_here, preferred_element_type=jnp.float32).astype(
        jnp.bfloat16
    )
    own_start = my_index * PICK_DEV
    own_rows = lax.dynamic_slice_in_dim(picked_rows, own_start, PICK_DEV, 0).astype(jnp.float32)
    attn_own = reduce_scatter_rows(
        jnp.dot(head_out, output_weight, preferred_element_type=jnp.float32).astype(jnp.bfloat16),
        ctx_size,
    )
    mixed_own = own_rows + attn_own
    normed_own = rms_scale(mixed_own, ffn_gain).astype(jnp.bfloat16)
    normed_ffn = lax.all_gather(normed_own, "ctx", axis=0, tiled=True)
    gate_proj = jnp.dot(normed_ffn, gate_weight, preferred_element_type=jnp.float32)
    up_proj = jnp.dot(normed_ffn, up_weight, preferred_element_type=jnp.float32)
    hidden = (jax.nn.silu(gate_proj) * up_proj).astype(jnp.bfloat16)
    ffn_own = reduce_scatter_rows(
        jnp.dot(hidden, down_weight, preferred_element_type=jnp.float32).astype(jnp.bfloat16),
        ctx_size,
    )
    scale_own = lax.dynamic_slice_in_dim(scales, own_start, PICK_DEV, 0)
    final_own = (own_rows + scale_own[:, None] * (attn_own + ffn_own)).astype(jnp.bfloat16)
    final_all = lax.all_gather(final_own, "ctx", axis=0, tiled=True)
    my_start = run_starts[my_index]
    rank_here = jnp.clip(my_start + slot_of, 0, picked_count - 1)
    inner_here = rank_here % PICK_DEV
    odd_here = inner_here % 2
    owner_here = (rank_here // PICK_DEV + odd_here * half_cycle) % ctx_size
    take_rows = owner_here * PICK_DEV + inner_here // 2 + odd_here * half_pick
    return jnp.where(pick_flags[:, None] == 1, final_all[take_rows], tokens)


def solution(mesh):
    in_specs = (
        P(("dp", "ctx"), None),
        P(("dp", "ctx")),
        P(("dp", "ctx")),
        P(),
        P(None, "ctx"),
        P(None, "ctx"),
        P(None, "ctx"),
        P("ctx", None),
        P(),
        P(None, "ctx"),
        P(None, "ctx"),
        P("ctx", None),
    )
    out_specs = P(("dp", "ctx"), None)
    return jax.shard_map(body, mesh=mesh, in_specs=in_specs, out_specs=out_specs, check_vma=False)
```

profile of v0, /device:TPU:2, one launch (start us, length us, event | category | flops | bytes accessed | tf_op | source)
XLA Modules:
  0.0 593.0 jit_solution(4322541667487675454)
XLA Ops:
  13.4 102.9 %all-gather.4.cloned.1.call-done = bf16[1024,4224]{1,0:T(8,128)(2,1)} async-done(((bf16[32,4224]{1,0:T(8,128)(2,1)}), bf16[1024,4224]{1,0:T(8,128)(2,1)}) %all-gather.4.cloned.1.call-update) | async-done | bytes 8650768 | tf_op jit(solution)/shard_map/all_gather | solution.py:82
  119.6 4.4 compare_select_fusion.5
  124.1 15.2 %select_select_fusion.1 = s32[512]{0:T(512)S(1)} fusion(pred[512]{0:T(512)(128)(4,1)S(1)} %get-tuple-element.31, pred[512]{0:T(512)(128)(4,1)S(1)} %get-tuple-element.30, pred[512]{0:T(512)(128)(4,1)S(1)} %get-tuple-element.29, pred[512]{0:T(512)(128)(4,1)S(1)} %get-tuple-element.28, pred[512]{0:T(512)(128)(4,1)S(1)} %get-tuple-element.27, ...), kind=kLoop, calls=%fused_computation.170 | loop fusion | flops 12800 | bytes 16996 | tf_op jit(solution)/shard_map/gather | solution.py:97
  139.4 7.7 %slice.81 = bf16[1024,4096]{1,0:T(8,128)(2,1)} slice(bf16[1024,4224]{1,0:T(8,128)(2,1)} %all-gather.4.cloned.1.call-done), slice={[0:1024], [0:4096]} | slice | bytes 16777216 | tf_op jit(solution)/shard_map/slice | solution.py:83
  147.2 13.0 %gather_fusion.2 = bf16[512,4096]{1,0:T(8,128)(2,1)} fusion(bf16[1024,4096]{1,0:T(8,128)(2,1)} %slice.81, s32[1024]{0:T(1024)S(1)} %pad_clamp_fusion.1), kind=kCustom, calls=%fused_computation.2 | custom fusion | bytes 8390656 | tf_op jit(solution)/shard_map/gather | solution.py:98
  162.5 3.2 fusion
  165.9 2.5 fusion.9
  169.3 5.8 all-to-all-start
  175.1 4.8 fusion.7
  179.9 6.9 %all-to-all-done = bf16[32,2,4,512]{3,2,1,0:T(4,128)(2,1)S(1)} async-done(((bf16[32,2,4,512]{3,2,1,0:T(4,128)(2,1)}), bf16[32,2,4,512]{3,2,1,0:T(4,128)(2,1)S(1)}, u32[]{:S(2)}, u32[]{:S(2)}) %all-to-all-start) | async-done | bytes 262176 | tf_op jit(solution)/shard_map/all_to_all | solution.py:112
  191.7 5.1 convolution_convert_fusion
  196.8 4.9 all-to-all-start.1
  201.8 95.8 %all-to-all-done.1 = bf16[32,16,4096]{2,1,0:T(8,128)(2,1)} async-done(((bf16[32,16,4096]{2,1,0:T(8,128)(2,1)}), bf16[32,16,4096]{2,1,0:T(8,128)(2,1)}, u32[]{:S(2)}, u32[]{:S(2)}) %all-to-all-start.1) | async-done | bytes 4194336 | tf_op jit(solution)/shard_map/all_to_all | solution.py:39
  297.5 2.9 convert_reduce_fusion.1
  303.2 77.5 %all-gather.6.cloned.1.call-done = bf16[512,4096]{1,0:T(8,128)(2,1)} async-done(((bf16[16,4096]{1,0:T(8,128)(2,1)}), bf16[512,4096]{1,0:T(8,128)(2,1)}) %all-gather.6.cloned.1.call-update) | async-done | bytes 4194320 | tf_op jit(solution)/shard_map/all_gather | solution.py:136
  380.7 5.6 fusion.79
  386.3 9.2 %convolution_convert_fusion.1 = bf16[512,4096]{1,0:T(8,128)(2,1)} fusion(bf16[352,4096]{1,0:T(8,128)(2,1)S(1)} %copy-done, bf16[512,4096]{1,0:T(8,128)(2,1)} %all-gather.6.cloned.1.call-done, bf16[4096,352]{0,1:T(8,128)(2,1)} %param.22, f32[512,352]{0,1:T(8,128)} %fusion.79), kind=kOutput, calls=%fused_computation.14 | convolution fusion | flops 2955968512 | bytes 14876672 | tf_op jit(solution)/shard_map/dot_general | solution.py:141
  395.5 5.9 %all-to-all-start.2 = ((bf16[32,16,4096]{2,1,0:T(8,128)(2,1)}), bf16[32,16,4096]{2,1,0:T(8,128)(2,1)}, u32[]{:S(2)}, u32[]{:S(2)}) async-start(bf16[32,16,4096]{2,1,0:T(8,128)(2,1)} %bitcast.59), calls=%async_computation.2 | async-start | bytes 8388608 | tf_op jit(solution)/shard_map/all_to_all | solution.py:39
  402.9 3.5 gather_fusion.3
  406.5 89.5 %all-to-all-done.2 = bf16[32,16,4096]{2,1,0:T(8,128)(2,1)} async-done(((bf16[32,16,4096]{2,1,0:T(8,128)(2,1)}), bf16[32,16,4096]{2,1,0:T(8,128)(2,1)}, u32[]{:S(2)}, u32[]{:S(2)}) %all-to-all-start.2) | async-done | bytes 4194336 | tf_op jit(solution)/shard_map/all_to_all | solution.py:39
  496.0 2.8 convert_reduce_fusion
  501.5 76.5 %all-gather.8.cloned.1.call-done = bf16[512,4096]{1,0:T(8,128)(2,1)} async-done(((bf16[16,4096]{1,0:T(8,128)(2,1)}), bf16[512,4096]{1,0:T(8,128)(2,1)}) %all-gather.8.cloned.1.call-update) | async-done | bytes 4194320 | tf_op jit(solution)/shard_map/all_gather | solution.py:146
  577.9 5.9 gather_fusion.5
  583.8 2.7 broadcast_select_fusion
  (66 shorter events, 25.3 us)
Async XLA Ops:
  6.5 379.8 %copy-start = (bf16[352,4096]{1,0:T(8,128)(2,1)S(1)}, bf16[352,4096]{1,0:T(8,128)(2,1)}, u32[]{:S(2)}) copy-start(bf16[352,4096]{1,0:T(8,128)(2,1)} %param.23) | copy-start | bytes 8650756
  6.5 109.8 %all-gather.4.cloned.1.call-start = ((), (), s32[]{:S(2)}) async-start(), calls=%async_computation.3 | async-start | bytes 8921088 | tf_op jit(solution)/shard_map/all_gather | solution.py:82
  160.2 5.5 copy-start.4
  162.5 3.5 copy-start.1
  169.3 17.6 %all-to-all-start = ((bf16[32,2,4,512]{3,2,1,0:T(4,128)(2,1)}), bf16[32,2,4,512]{3,2,1,0:T(4,128)(2,1)S(1)}, u32[]{:S(2)}, u32[]{:S(2)}) async-start(bf16[32,2,4,512]{3,2,1,0:T(4,128)(2,1)} %bitcast.42), calls=%async_computation | async-start | bytes 524288 | tf_op jit(solution)/shard_map/all_to_all | solution.py:112
  190.5 1.0 copy-start.2
  196.8 100.7 %all-to-all-start.1 = ((bf16[32,16,4096]{2,1,0:T(8,128)(2,1)}), bf16[32,16,4096]{2,1,0:T(8,128)(2,1)}, u32[]{:S(2)}, u32[]{:S(2)}) async-start(bf16[32,16,4096]{2,1,0:T(8,128)(2,1)} %bitcast.58), calls=%async_computation.1 | async-start | bytes 8388608 | tf_op jit(solution)/shard_map/all_to_all | solution.py:39
  201.7 99.8 %copy-start.3 = (f32[4096]{0:T(1024)S(1)}, f32[4096]{0:T(1024)}, u32[]{:S(2)}) copy-start(f32[4096]{0:T(1024)} %param.20) | copy-start | bytes 49156
  201.7 179.0 %all-gather.6.cloned.1.call-start = ((), (), s32[]{:S(2)}) async-start(), calls=%async_computation.4 | async-start | bytes 4325376 | tf_op jit(solution)/shard_map/all_gather | solution.py:136
  395.5 100.5 %all-to-all-start.2 = ((bf16[32,16,4096]{2,1,0:T(8,128)(2,1)}), bf16[32,16,4096]{2,1,0:T(8,128)(2,1)}, u32[]{:S(2)}, u32[]{:S(2)}) async-start(bf16[32,16,4096]{2,1,0:T(8,128)(2,1)} %bitcast.59), calls=%async_computation.2 | async-start | bytes 8388608 | tf_op jit(solution)/shard_map/all_to_all | solution.py:39
  401.5 176.5 %all-gather.8.cloned.1.call-start = ((), (), s32[]{:S(2)}) async-start(), calls=%async_computation.5 | async-start | bytes 4325376 | tf_op jit(solution)/shard_map/all_gather | solution.py:146
Sparse Core Ops, SparseCore 0:
  13.5 102.8 all-gather.3
  303.3 77.3 all-gather.5
  500.7 77.2 all-gather.7
where the time goes:
time: 594 us; the launch traced here: 593 us
  waiting for transfers between devices  449 us (76%)
  other arithmetic  43.2 us (7%)
  local copies, waits for them, and re-layouts  42.8 us (7%)
  matrix products  27.6 us (5%)
  starting transfers between devices  16.9 us (3%)
  between operations  13.4 us (2%)
    all_to_all x2, waiting for transfers between devices, reduce_scatter_rows(): lax.all_to_all(partial.reshape(ctx_size, rows // ctx_size, width), 'ctx',...  185 us
    all_gather x1, waiting for transfers between devices, body(): all_packed = lax.all_gather(packed, 'ctx', axis=0, tiled=True)  103 us
    all_gather x1, waiting for transfers between devices, body(): normed_ffn = lax.all_gather(normed_own, 'ctx', axis=0, tiled=True)  77.5 us
    all_gather x1, waiting for transfers between devices, body(): final_all = lax.all_gather(final_own, 'ctx', axis=0, tiled=True)  76.5 us
    gather x3, other arithmetic, body(): flat_row = source * MOST + rank_ids - run_starts[source]  19.8 us
    gather x1, local copies, waits for them, and re-layouts, body(): picked_rows = all_rows[flat_row]  13 us
  transfers between devices with their start and end apart: 6, of which 6 were waited for; matrix products, arithmetic and copies ran while one was open for 2% of the time, Pallas kernels for 0%

commit v1 on v0

--- a/solution.py
+++ b/solution.py
@@ -133,7 +133,11 @@
     )
     mixed_own = own_rows + attn_own
     normed_own = rms_scale(mixed_own, ffn_gain).astype(jnp.bfloat16)
-    normed_ffn = lax.all_gather(normed_own, "ctx", axis=0, tiled=True)
+    devices = lax.axis_size("ctx")
+    repeats = [devices if d == 0 else 1 for d in range(normed_own.ndim)]
+    normed_ffn = lax.all_to_all(
+        jnp.tile(normed_own, repeats), "ctx", split_axis=0, concat_axis=0, tiled=True
+    )
     gate_proj = jnp.dot(normed_ffn, gate_weight, preferred_element_type=jnp.float32)
     up_proj = jnp.dot(normed_ffn, up_weight, preferred_element_type=jnp.float32)
     hidden = (jax.nn.silu(gate_proj) * up_proj).astype(jnp.bfloat16)

time: 594 us -> 618 us (1.040)
  blocking collectives: 0 us -> 100 us
  waiting for transfers between devices: 449 us -> 375 us
    all_to_all x0 -> x1, blocking collectives: none -> 100 us  [body(): lax.all_to_all(jnp.tile(normed_own, repeats), 'ctx', split_axis=0, concat...]
    all_gather x1 -> x0, waiting for transfers between devices: 77.5 us -> none  [body(): normed_ffn = lax.all_gather(normed_own, 'ctx', axis=0, tiled=True)]
  transfers between devices with their start and end apart: 6 -> 5, of which waited for: 6 -> 5; matrix products, arithmetic and copies ran while one was open for 2% -> 2% of each run, Pallas kernels for 0% -> 0%
where the time goes in v1:
time: 618 us; the launch traced here: 617 us
  waiting for transfers between devices  375 us (61%)
  blocking collectives  100 us (16%)
  local copies, waits for them, and re-layouts  45.3 us (7%)
  other arithmetic  42.5 us (7%)
  matrix products  24.6 us (4%)
  starting transfers between devices  16.1 us (3%)
  between operations  13.7 us (2%)
    all_to_all x2, waiting for transfers between devices, reduce_scatter_rows(): lax.all_to_all(partial.reshape(ctx_size, rows // ctx_size, width), 'ctx',...  187 us
    all_gather x1, waiting for transfers between devices, body(): all_packed = lax.all_gather(packed, 'ctx', axis=0, tiled=True)  103 us
    all_to_all x1, blocking collectives, body(): lax.all_to_all(jnp.tile(normed_own, repeats), 'ctx', split_axis=0, concat...  100 us
    all_gather x1, waiting for transfers between devices, body(): final_all = lax.all_gather(final_own, 'ctx', axis=0, tiled=True)  77.3 us
    gather x3, other arithmetic, body(): flat_row = source * MOST + rank_ids - run_starts[source]  19.8 us
    gather x1, local copies, waits for them, and re-layouts, body(): picked_rows = all_rows[flat_row]  13 us
  transfers between devices with their start and end apart: 5, of which 5 were waited for; matrix products, arithmetic and copies ran while one was open for 2% of the time, Pallas kernels for 0%

profile of v1, /device:TPU:2, one launch (start us, length us, event | category | flops | bytes accessed | tf_op | source)
XLA Modules:
  0.0 616.9 jit_solution(11148454472538763149)
XLA Ops:
  13.4 102.9 %all-gather.3.cloned.1.call-done = bf16[1024,4224]{1,0:T(8,128)(2,1)} async-done(((bf16[32,4224]{1,0:T(8,128)(2,1)}), bf16[1024,4224]{1,0:T(8,128)(2,1)}) %all-gather.3.cloned.1.call-update) | async-done | bytes 8650768 | tf_op jit(solution)/shard_map/all_gather | solution.py:82
  119.6 4.4 compare_select_fusion.5
  124.1 15.2 %select_select_fusion.1 = s32[512]{0:T(512)S(1)} fusion(pred[512]{0:T(512)(128)(4,1)S(1)} %get-tuple-element.31, pred[512]{0:T(512)(128)(4,1)S(1)} %get-tuple-element.30, pred[512]{0:T(512)(128)(4,1)S(1)} %get-tuple-element.29, pred[512]{0:T(512)(128)(4,1)S(1)} %get-tuple-element.28, pred[512]{0:T(512)(128)(4,1)S(1)} %get-tuple-element.27, ...), kind=kLoop, calls=%fused_computation.170 | loop fusion | flops 12800 | bytes 16996 | tf_op jit(solution)/shard_map/gather | solution.py:97
  139.4 7.7 %slice.81 = bf16[1024,4096]{1,0:T(8,128)(2,1)} slice(bf16[1024,4224]{1,0:T(8,128)(2,1)} %all-gather.3.cloned.1.call-done), slice={[0:1024], [0:4096]} | slice | bytes 16777216 | tf_op jit(solution)/shard_map/slice | solution.py:83
  147.2 13.0 %gather_fusion.2 = bf16[512,4096]{1,0:T(8,128)(2,1)} fusion(bf16[1024,4096]{1,0:T(8,128)(2,1)} %slice.81, s32[1024]{0:T(1024)S(1)} %pad_clamp_fusion.1), kind=kCustom, calls=%fused_computation.2 | custom fusion | bytes 8390656 | tf_op jit(solution)/shard_map/gather | solution.py:98
  162.5 3.2 fusion
  165.9 2.5 fusion.9
  169.3 5.8 all-to-all-start
  175.1 4.8 fusion.7
  179.9 6.9 %all-to-all-done = bf16[32,2,4,512]{3,2,1,0:T(4,128)(2,1)S(1)} async-done(((bf16[32,2,4,512]{3,2,1,0:T(4,128)(2,1)}), bf16[32,2,4,512]{3,2,1,0:T(4,128)(2,1)S(1)}, u32[]{:S(2)}, u32[]{:S(2)}) %all-to-all-start) | async-done | bytes 262176 | tf_op jit(solution)/shard_map/all_to_all | solution.py:112
  191.7 5.1 convolution_convert_fusion
  196.8 4.9 all-to-all-start.1
  201.7 95.8 %all-to-all-done.1 = bf16[32,16,4096]{2,1,0:T(8,128)(2,1)} async-done(((bf16[32,16,4096]{2,1,0:T(8,128)(2,1)}), bf16[32,16,4096]{2,1,0:T(8,128)(2,1)}, u32[]{:S(2)}, u32[]{:S(2)}) %all-to-all-start.1) | async-done | bytes 4194336 | tf_op jit(solution)/shard_map/all_to_all | solution.py:39
  297.5 2.9 convert_reduce_fusion.1
  303.0 100.2 %all_to_all.24 = bf16[32,16,4096]{2,1,0:T(8,128)(2,1)S(1)} all-to-all(bf16[32,16,4096]{2,1,0:T(8,128)(2,1)S(1)} %tile.2), channel_id=1, replica_groups=mesh['dp'=8,'ctx'=32] {'ctx'}, dimensions={0} | all-to-all | bytes 8388608 | tf_op jit(solution)/shard_map/all_to_all | solution.py:138
  405.2 2.6 fusion.79
  407.8 9.2 %convolution_convert_fusion.1 = bf16[512,4096]{1,0:T(8,128)(2,1)} fusion(bf16[352,4096]{1,0:T(8,128)(2,1)S(1)} %copy-done, bf16[512,4096]{1,0:T(8,128)(2,1)} %bitcast.62, bf16[4096,352]{0,1:T(8,128)(2,1)} %param.22, f32[512,352]{0,1:T(8,128)} %fusion.79), kind=kOutput, calls=%fused_computation.14 | convolution fusion | flops 2955968512 | bytes 14876672 | tf_op jit(solution)/shard_map/dot_general | solution.py:145
  416.9 5.2 all-to-all-start.3
  423.6 3.5 gather_fusion.3
  427.2 91.5 %all-to-all-done.3 = bf16[32,16,4096]{2,1,0:T(8,128)(2,1)} async-done(((bf16[32,16,4096]{2,1,0:T(8,128)(2,1)}), bf16[32,16,4096]{2,1,0:T(8,128)(2,1)}, u32[]{:S(2)}, u32[]{:S(2)}) %all-to-all-start.3) | async-done | bytes 4194336 | tf_op jit(solution)/shard_map/all_to_all | solution.py:39
  518.6 2.8 convert_reduce_fusion
  524.1 77.3 %all-gather.5.cloned.1.call-done = bf16[512,4096]{1,0:T(8,128)(2,1)} async-done(((bf16[16,4096]{1,0:T(8,128)(2,1)}), bf16[512,4096]{1,0:T(8,128)(2,1)}) %all-gather.5.cloned.1.call-update) | async-done | bytes 4194320 | tf_op jit(solution)/shard_map/all_gather | solution.py:150
  601.5 5.9 gather_fusion.5
  607.4 2.7 broadcast_select_fusion
  (69 shorter events, 27.1 us)
Async XLA Ops:
  6.5 401.2 %copy-start = (bf16[352,4096]{1,0:T(8,128)(2,1)S(1)}, bf16[352,4096]{1,0:T(8,128)(2,1)}, u32[]{:S(2)}) copy-start(bf16[352,4096]{1,0:T(8,128)(2,1)} %param.23) | copy-start | bytes 8650756
  6.5 109.8 %all-gather.3.cloned.1.call-start = ((), (), s32[]{:S(2)}) async-start(), calls=%async_computation.4 | async-start | bytes 8921088 | tf_op jit(solution)/shard_map/all_gather | solution.py:82
  160.2 5.5 copy-start.6
  162.5 3.5 copy-start.1
  169.3 17.6 %all-to-all-start = ((bf16[32,2,4,512]{3,2,1,0:T(4,128)(2,1)}), bf16[32,2,4,512]{3,2,1,0:T(4,128)(2,1)S(1)}, u32[]{:S(2)}, u32[]{:S(2)}) async-start(bf16[32,2,4,512]{3,2,1,0:T(4,128)(2,1)} %bitcast.42), calls=%async_computation | async-start | bytes 524288 | tf_op jit(solution)/shard_map/all_to_all | solution.py:112
  190.5 1.0 copy-start.3
  196.8 100.7 %all-to-all-start.1 = ((bf16[32,16,4096]{2,1,0:T(8,128)(2,1)}), bf16[32,16,4096]{2,1,0:T(8,128)(2,1)}, u32[]{:S(2)}, u32[]{:S(2)}) async-start(bf16[32,16,4096]{2,1,0:T(8,128)(2,1)} %bitcast.59), calls=%async_computation.1 | async-start | bytes 8388608 | tf_op jit(solution)/shard_map/all_to_all | solution.py:39
  201.7 99.8 %copy-start.4 = (f32[4096]{0:T(1024)S(1)}, f32[4096]{0:T(1024)}, u32[]{:S(2)}) copy-start(f32[4096]{0:T(1024)} %param.20) | copy-start | bytes 49156
  303.0 102.2 %copy-start.5 = (bf16[4096,352]{0,1:T(8,128)(2,1)S(1)}, bf16[4096,352]{0,1:T(8,128)(2,1)}, u32[]{:S(2)}) copy-start(bf16[4096,352]{0,1:T(8,128)(2,1)} %param.21) | copy-start | bytes 8650756
  403.2 1.9 copy-start.2
  416.9 101.7 %all-to-all-start.3 = ((bf16[32,16,4096]{2,1,0:T(8,128)(2,1)}), bf16[32,16,4096]{2,1,0:T(8,128)(2,1)}, u32[]{:S(2)}, u32[]{:S(2)}) async-start(bf16[32,16,4096]{2,1,0:T(8,128)(2,1)} %bitcast.60), calls=%async_computation.3 | async-start | bytes 8388608 | tf_op jit(solution)/shard_map/all_to_all | solution.py:39
  422.1 179.3 %all-gather.5.cloned.1.call-start = ((), (), s32[]{:S(2)}) async-start(), calls=%async_computation.5 | async-start | bytes 4325376 | tf_op jit(solution)/shard_map/all_gather | solution.py:150
Sparse Core Ops, SparseCore 0:
  13.5 102.8 all-gather.2
  523.3 78.1 all-gather.4
